TPU v7x, 32 devices: a whole 2x2x4 slice. The times are simulated.
32 devices in a mesh: col: 8 (over y, x, core), row: 4 (over z).
Axes of the slice: x: 2, y: 2, z: 4, core: 2. Of those that a mesh axis runs over, the one named last changes fastest.
Arguments:
- rhs: bfloat16 [6, 8, 4, 128, 512], P(None, 'col', 'row'), may hold values from -6 to 6
- diag_inv: bfloat16 [6, 8, 4, 128, 128], P(None, 'col', 'row'), may hold values from -0.5 to 0.5
- factor: bfloat16 [5, 8, 4, 8, 2, 128, 128], P(None, 'col', 'row'), may hold values from -0.1875 to 0.1875
- columns: int32 [5, 8, 4, 8, 2], P(None, 'col', 'row'), may hold values from 0 to 3, as said below
Outputs:
- solution: bfloat16 [6, 8, 4, 128, 512], P(None, 'col', 'row')
Inputs may be any that keep to these rules, and one draw needn't show every extreme that they name: The 2 entries of columns for one factor row block and one column owner are distinct.
All inputs are finite; a program needn't handle non-finite values.
Results may differ from a plain program's by a relative error of at most 0.025.
Values may be sent and summed in bfloat16 or wider, within the bound.
A program may use at most 128 MiB of HBM per device.

v0:
```python
import jax
import jax.numpy as jnp
from jax import lax
from jax.sharding import PartitionSpec as P


def solve_block(inverse, remainder):
    product = jnp.dot(
        inverse.astype(jnp.float32),
        remainder,
        precision=lax.Precision.HIGHEST,
        preferred_element_type=jnp.float32,
    )
    return product.astype(jnp.bfloat16)


def local_terms(blocks, selected, panels):
    chosen = jnp.take(panels, selected, axis=0)
    return jnp.einsum("tmab,tmbn->tan", blocks, chosen, preferred_element_type=jnp.float32)


def on_device(rhs, diag_inv, factor, columns):
    step_count = rhs.shape[0]
    solved = []
    remainder = rhs[0, 0, 0].astype(jnp.float32)
    for step_index in range(step_count):
        current = solve_block(diag_inv[step_index, 0, 0], remainder)
        solved.append(current)
        if step_index + 1 < step_count:
            panels = lax.all_gather(current[None], "row", axis=0, tiled=True)
            contrib = local_terms(factor[step_index, 0, 0], columns[step_index, 0, 0], panels)
            summed = lax.psum_scatter(
                contrib.astype(jnp.bfloat16), "col", scatter_dimension=0, tiled=True
            ).astype(jnp.float32)
            remainder = rhs[step_index + 1, 0, 0].astype(jnp.float32) - summed[0]
    return jnp.stack(solved)[:, None, None]


def solution(mesh):
    return jax.shard_map(
        on_device,
        mesh=mesh,
        in_specs=(
            P(None, "col", "row", None, None),
            P(None, "col", "row", None, None),
            P(None, "col", "row", None, None, None, None),
            P(None, "col", "row", None, None),
        ),
        out_specs=P(None, "col", "row", None, None),
        check_vma=False,
    )
```

profile of v0, /device:TPU:0, one launch (start us, length us, event | category | flops | bytes accessed | tf_op | source)
XLA Modules:
  0.0 323.3 jit_solution(17389565286703489499)
XLA Ops:
  6.5 0.7 compare_select_fusion
  7.3 0.8 compare_and_fusion
  8.0 1.8 bitcast_dynamic-update-slice_fusion.4
  9.8 17.4 %all-gather = bf16[512,512]{1,0:T(8,128)(2,1)S(1)} all-gather(bf16[128,512]{1,0:T(8,128)(2,1)S(1)} %get-tuple-element.22), channel_id=2, replica_groups=mesh['col'=8,'row'=4] {'row'}, dimensions={0}, use_global_device_ids=true | all-gather | bytes 655360 | tf_op jit(solution)/shard_map/all_gather | solution.py:30
  27.3 0.7 gather_fusion
  28.0 2.4 copy.34
  30.5 3.5 %fusion.25 = bf16[8,128,512]{1,2,0:T(8,128)(2,1)} fusion(bf16[8,2,128,512]{2,3,1,0:T(8,128)(2,1)} %bitcast.206, pred[8,2]{1,0:T(8,128)(4,1)S(1)} %copy.32, bf16[5,1,1,8,2,128,128]{6,5,4,3,2,1,0:T(8,128)(2,1)} %param.8), kind=kOutput, calls=%fused_computation.25 | convolution fusion | flops 270008320 | bytes 3670032 | tf_op jit(solution)/shard_map/tmab,tmbn->tan/dot_general | solution.py:19
  34.5 37.4 %reduce-scatter.6.cloned.1.call-done = bf16[1,128,512]{1,2,0:T(8,128)(2,1)} async-done(((bf16[8,128,512]{1,2,0:T(8,128)(2,1)}), bf16[1,128,512]{1,2,0:T(8,128)(2,1)}) %reduce-scatter.6.cloned.1.call-update) | async-done | bytes 131088 | tf_op jit(solution)/shard_map/reduce_scatter | solution.py:32
  72.0 1.9 bitcast_dynamic-update-slice_fusion.3
  73.8 15.4 %all-gather.1 = bf16[512,512]{1,0:T(8,128)(2,1)S(1)} all-gather(bf16[128,512]{1,0:T(8,128)(2,1)S(1)} %bitcast.211), channel_id=3, replica_groups=mesh['col'=8,'row'=4] {'row'}, dimensions={0}, use_global_device_ids=true | all-gather | bytes 655360 | tf_op jit(solution)/shard_map/all_gather | solution.py:30
  89.2 0.7 gather_fusion.1
  89.9 2.4 copy.39
  92.3 3.4 %fusion.28 = bf16[8,128,512]{1,2,0:T(8,128)(2,1)} fusion(bf16[8,2,128,512]{2,3,1,0:T(8,128)(2,1)} %bitcast.207, pred[8,2]{1,0:T(8,128)(4,1)S(1)} %copy.37, bf16[5,1,1,8,2,128,128]{6,5,4,3,2,1,0:T(8,128)(2,1)} %param.8), kind=kOutput, calls=%fused_computation.26 | convolution fusion | flops 270008320 | bytes 3670032 | tf_op jit(solution)/shard_map/tmab,tmbn->tan/dot_general | solution.py:19
  96.1 36.6 %reduce-scatter.8.cloned.1.call-done = bf16[1,128,512]{1,2,0:T(8,128)(2,1)} async-done(((bf16[8,128,512]{1,2,0:T(8,128)(2,1)}), bf16[1,128,512]{1,2,0:T(8,128)(2,1)}) %reduce-scatter.8.cloned.1.call-update) | async-done | bytes 131088 | tf_op jit(solution)/shard_map/reduce_scatter | solution.py:32
  132.8 1.9 bitcast_dynamic-update-slice_fusion.2
  134.7 15.3 %all-gather.2 = bf16[512,512]{1,0:T(8,128)(2,1)S(1)} all-gather(bf16[128,512]{1,0:T(8,128)(2,1)S(1)} %bitcast.212), channel_id=4, replica_groups=mesh['col'=8,'row'=4] {'row'}, dimensions={0}, use_global_device_ids=true | all-gather | bytes 655360 | tf_op jit(solution)/shard_map/all_gather | solution.py:30
  150.0 0.7 gather_fusion.2
  150.7 2.4 copy.44
  153.1 3.4 %fusion.31 = bf16[8,128,512]{1,2,0:T(8,128)(2,1)} fusion(bf16[8,2,128,512]{2,3,1,0:T(8,128)(2,1)} %bitcast.208, pred[8,2]{1,0:T(8,128)(4,1)S(1)} %copy.42, bf16[5,1,1,8,2,128,128]{6,5,4,3,2,1,0:T(8,128)(2,1)} %param.8), kind=kOutput, calls=%fused_computation.27 | convolution fusion | flops 270008320 | bytes 3670032 | tf_op jit(solution)/shard_map/tmab,tmbn->tan/dot_general | solution.py:19
  156.9 36.6 %reduce-scatter.10.cloned.1.call-done = bf16[1,128,512]{1,2,0:T(8,128)(2,1)} async-done(((bf16[8,128,512]{1,2,0:T(8,128)(2,1)}), bf16[1,128,512]{1,2,0:T(8,128)(2,1)}) %reduce-scatter.10.cloned.1.call-update) | async-done | bytes 131088 | tf_op jit(solution)/shard_map/reduce_scatter | solution.py:32
  193.5 1.9 bitcast_dynamic-update-slice_fusion.1
  195.4 15.4 %all-gather.3 = bf16[512,512]{1,0:T(8,128)(2,1)S(1)} all-gather(bf16[128,512]{1,0:T(8,128)(2,1)S(1)} %bitcast.213), channel_id=5, replica_groups=mesh['col'=8,'row'=4] {'row'}, dimensions={0}, use_global_device_ids=true | all-gather | bytes 655360 | tf_op jit(solution)/shard_map/all_gather | solution.py:30
  210.8 0.7 gather_fusion.3
  211.5 2.4 copy.49
  213.8 3.4 %fusion.34 = bf16[8,128,512]{1,2,0:T(8,128)(2,1)} fusion(bf16[8,2,128,512]{2,3,1,0:T(8,128)(2,1)} %bitcast.209, pred[8,2]{1,0:T(8,128)(4,1)S(1)} %copy.47, bf16[5,1,1,8,2,128,128]{6,5,4,3,2,1,0:T(8,128)(2,1)} %param.8), kind=kOutput, calls=%fused_computation.28 | convolution fusion | flops 270008320 | bytes 3670032 | tf_op jit(solution)/shard_map/tmab,tmbn->tan/dot_general | solution.py:19
  217.7 36.5 %reduce-scatter.12.cloned.1.call-done = bf16[1,128,512]{1,2,0:T(8,128)(2,1)} async-done(((bf16[8,128,512]{1,2,0:T(8,128)(2,1)}), bf16[1,128,512]{1,2,0:T(8,128)(2,1)}) %reduce-scatter.12.cloned.1.call-update) | async-done | bytes 131088 | tf_op jit(solution)/shard_map/reduce_scatter | solution.py:32
  254.2 1.9 bitcast_dynamic-update-slice_fusion
  256.1 15.4 %all-gather.4 = bf16[512,512]{1,0:T(8,128)(2,1)S(1)} all-gather(bf16[128,512]{1,0:T(8,128)(2,1)S(1)} %bitcast.214), channel_id=6, replica_groups=mesh['col'=8,'row'=4] {'row'}, dimensions={0}, use_global_device_ids=true | all-gather | bytes 655360 | tf_op jit(solution)/shard_map/all_gather | solution.py:30
  272.2 2.4 copy.54
  274.5 3.4 %fusion.37 = bf16[8,128,512]{1,2,0:T(8,128)(2,1)} fusion(bf16[8,2,128,512]{2,3,1,0:T(8,128)(2,1)} %bitcast.210, pred[8,2]{1,0:T(8,128)(4,1)S(1)} %copy.52, bf16[5,1,1,8,2,128,128]{6,5,4,3,2,1,0:T(8,128)(2,1)} %param.8), kind=kOutput, calls=%fused_computation.29 | convolution fusion | flops 270008320 | bytes 3670032 | tf_op jit(solution)/shard_map/tmab,tmbn->tan/dot_general | solution.py:19
  278.1 36.8 %reduce-scatter.14.cloned.1.call-done = bf16[1,128,512]{1,2,0:T(8,128)(2,1)} async-done(((bf16[8,128,512]{1,2,0:T(8,128)(2,1)}), bf16[1,128,512]{1,2,0:T(8,128)(2,1)}) %reduce-scatter.14.cloned.1.call-update) | async-done | bytes 131088 | tf_op jit(solution)/shard_map/reduce_scatter | solution.py:32
  314.9 1.9 fusion.41
  (41 shorter events, 2.9 us)
Async XLA Ops:
  6.5 65.4 %reduce-scatter.6.cloned.1.call-start = ((), (), s32[]{:S(2)}) async-start(), calls=%async_computation.5 | async-start | bytes 1179648 | tf_op jit(solution)/shard_map/reduce_scatter | solution.py:32
  30.5 3.6 %copy-start = (bf16[6,1,1,128,512]{4,3,2,1,0:T(8,128)(2,1)S(1)}, bf16[6,1,1,128,512]{4,3,2,1,0:T(8,128)(2,1)}, u32[]{:S(2)}) copy-start(bf16[6,1,1,128,512]{4,3,2,1,0:T(8,128)(2,1)} %param.6) | copy-start | bytes 2359300
  34.0 38.0 %copy-start.1 = (bf16[6,1,1,128,128]{4,3,2,1,0:T(8,128)(2,1)S(1)}, bf16[6,1,1,128,128]{4,3,2,1,0:T(8,128)(2,1)}, u32[]{:S(2)}) copy-start(bf16[6,1,1,128,128]{4,3,2,1,0:T(8,128)(2,1)} %param.7) | copy-start | bytes 589828
  34.0 98.8 %reduce-scatter.8.cloned.1.call-start = ((), (), s32[]{:S(2)}) async-start(), calls=%async_computation.6 | async-start | bytes 1179648 | tf_op jit(solution)/shard_map/reduce_scatter | solution.py:32
  95.7 97.8 %reduce-scatter.10.cloned.1.call-start = ((), (), s32[]{:S(2)}) async-start(), calls=%async_computation.7 | async-start | bytes 1179648 | tf_op jit(solution)/shard_map/reduce_scatter | solution.py:32
  156.5 97.7 %reduce-scatter.12.cloned.1.call-start = ((), (), s32[]{:S(2)}) async-start(), calls=%async_computation.8 | async-start | bytes 1179648 | tf_op jit(solution)/shard_map/reduce_scatter | solution.py:32
  217.3 97.6 %reduce-scatter.14.cloned.1.call-start = ((), (), s32[]{:S(2)}) async-start(), calls=%async_computation.9 | async-start | bytes 1179648 | tf_op jit(solution)/shard_map/reduce_scatter | solution.py:32
Sparse Core Ops, SparseCore 0:
  34.1 37.7 reduce-scatter.5
  95.8 36.9 reduce-scatter.7
  156.6 36.8 reduce-scatter.9
  217.4 36.7 reduce-scatter.11
  278.1 36.7 reduce-scatter.13
where the time goes:
time: 324 us; the launch traced here: 323 us
  waiting for transfers between devices  184 us (57%)
  blocking collectives  78.8 us (24%)
  matrix products  28.3 us (9%)
  local copies, waits for them, and re-layouts  17.3 us (5%)
  between operations  13.3 us (4%)
    reduce_scatter x5, waiting for transfers between devices, on_device(): lax.psum_scatter(contrib.astype(jnp.bfloat16), 'col', scatter_dimension=0...  184 us
    all_gather x5, blocking collectives, on_device(): panels = lax.all_gather(current[None], 'row', axis=0, tiled=True)  78.8 us
    dot_general x5, matrix products, local_terms(): jnp.einsum('tmab,tmbn->tan', blocks, chosen, preferred_element_type=jnp.f...  17.1 us
    gather x10, local copies, waits for them, and re-layouts, local_terms(): chosen = jnp.take(panels, selected, axis=0)  15.3 us
    dot_general x6, matrix products, solve_block(): jnp.dot(inverse.astype(jnp.float32), remainder, precision=lax.Precision.H...  11.2 us
  transfers between devices with their start and end apart: 5, of which 5 were waited for; matrix products, arithmetic and copies ran while one was open for 1% of the time, Pallas kernels for 0%

commit v1 on v0

v1 whole, which is shorter than its diff:
```python
import functools

import jax
import jax.numpy as jnp
from jax import lax
from jax.experimental import pallas as pl
from jax.experimental.pallas import tpu as pltpu
from jax.sharding import PartitionSpec as P

MESH = pl.DeviceIdType.MESH
CHUNKS = 2


def kernel(n_col, n_row, rhs, diag, fac, cols, cols_hbm, out, *scratch):
    steps, rows, width = rhs.shape[0], rhs.shape[3], rhs.shape[4]
    slots = fac.shape[4]
    chips = n_col // 2
    half = width // 2
    wide = half // CHUNKS
    links = steps - 1

    (rv, dv, fv, cp, own, sent, landed, last,
     in_loc, in_send, in_recv, z_send, z_recv, c_send, c_recv,
     o_loc, o_send, o_recv) = scratch[:18]
    panels = scratch[18:]

    col = lax.axis_index("col")
    row = lax.axis_index("row")
    core = lax.rem(col, 2)
    chip = lax.div(col, 2)
    partner = col + 1 - 2 * core
    mine = pl.ds(pl.multiple_of(core * half, half), half)
    theirs = pl.ds(pl.multiple_of((1 - core) * half, half), half)

    def to(c, r):
        return {"col": c, "row": r}

    def spans(total):
        return [pl.ds(0, 1), pl.ds(1, total - 1)]

    local = {}
    for g in range(2):
        a, b = spans(steps)[g], spans(links)[g]
        local["rhs", g] = pltpu.make_async_copy(rhs.at[a, 0, 0, :, mine], rv.at[a, 0], in_loc.at[0, g])
        local["diag", g] = pltpu.make_async_copy(diag.at[a, 0, 0], dv.at[a, 0], in_loc.at[1, g])
        local["fac", g] = pltpu.make_async_copy(fac.at[b, 0, 0], fv.at[b, 0], in_loc.at[2, g])
    for c in local.values():
        c.start()

    barrier = pltpu.get_barrier_semaphore()
    pl.semaphore_signal(barrier, inc=1, device_id=to(partner, row), device_id_type=MESH)
    for d in range(1, n_row):
        pl.semaphore_signal(barrier, inc=1, device_id=to(col, lax.rem(row + d, n_row)), device_id_type=MESH)
    for d in range(1, chips):
        other = lax.rem(chip + d, chips) * 2 + core
        pl.semaphore_signal(barrier, inc=1, device_id=to(other, row), device_id_type=MESH)
    pl.semaphore_wait(barrier, 1 + n_row - 1 + chips - 1)

    def remote(src, dst, send, recv, device):
        return pltpu.make_async_remote_copy(
            src_ref=src, dst_ref=dst, send_sem=send, recv_sem=recv,
            device_id=device, device_id_type=MESH)

    pair = to(partner, row)
    cross = {}
    for g in range(2):
        a, b = spans(steps)[g], spans(links)[g]
        cross["rhs", g] = remote(rhs.at[a, 0, 0, :, theirs], rv.at[a, 1], in_send.at[0, g], in_recv.at[0, g], pair)
        cross["diag", g] = remote(diag.at[a, 0, 0], dv.at[a, 1], in_send.at[1, g], in_recv.at[1, g], pair)
        cross["fac", g] = remote(fac.at[b, 0, 0], fv.at[b, 1], in_send.at[2, g], in_recv.at[2, g], pair)
        if g == 0:
            cross["cols", g] = remote(cols_hbm, cp, in_send.at[3, g], in_recv.at[3, g], pair)
    for c in cross.values():
        c.start()

    def arrived(name, g):
        if (name, g) in local:
            local[name, g].wait()
        cross[name, g].wait_recv()

    def part(ch):
        return pl.ds(ch * wide, wide)

    def z_copy(s, ch, d):
        buf = panels[s * CHUNKS + ch]
        return remote(buf.at[row], buf.at[row], z_send.at[s, ch, d - 1], z_recv.at[s, ch, d - 1],
                      to(col, lax.rem(row + d, n_row)))

    def c_copy(s, ch, d):
        other = lax.rem(chip + d, chips) * 2 + core
        return remote(sent.at[s, ch, d - 1], landed.at[s, ch, d - 1], c_send.at[s, ch, d - 1],
                      c_recv.at[s, ch, d - 1], to(other, row))

    def held(s, ch):
        return panels[s * CHUNKS + ch].at[row] if s < links else last.at[ch]

    def out_copies(s, ch):
        span = pl.ds(pl.multiple_of(core * half + ch * wide, wide), wide)
        src = held(s, ch)
        keep = pltpu.make_async_copy(src.at[0], out.at[s, 0, 0, :, span], o_loc.at[s, ch])
        give = remote(src.at[1], out.at[s, 0, 0, :, span], o_send.at[s, ch], o_recv.at[s, ch], pair)
        return keep, give

    def solve(s, ch):
        if s > 0:
            for d in range(1, chips):
                c_copy(s - 1, ch, d).wait_recv()
        for k in range(2):
            block = dv[s, k]
            right = rv[s, k, :, part(ch)]
            if s == 0:
                x = jnp.dot(block, right, preferred_element_type=jnp.float32)
            else:
                total = own[ch, k]
                for d in range(1, chips):
                    total = total + landed[s - 1, ch, d - 1, k].astype(jnp.float32)
                rem = right.astype(jnp.float32) - total
                high = rem.astype(jnp.bfloat16)
                low = (rem - high.astype(jnp.float32)).astype(jnp.bfloat16)
                x = jnp.dot(jnp.concatenate([block, block], axis=1),
                            jnp.concatenate([high, low], axis=0),
                            preferred_element_type=jnp.float32)
            x = x.astype(jnp.bfloat16)
            if s < links:
                panels[s * CHUNKS + ch][row, k] = x
            else:
                last[ch, k] = x
        if s < links:
            for d in range(1, n_row):
                z_copy(s, ch, d).start()
        for c in out_copies(s, ch):
            c.start()

    def term(s, ch, other, k):
        buf = panels[s * CHUNKS + ch]
        t = other * 2 + (core if k == 0 else 1 - core)
        left, right = [], []
        for slot, index in ((0, cols), (1, cp)):
            for m in range(slots):
                left.append(fv[s, slot, t, m])
                right.append(buf[index[s, 0, 0, t, m], slot])
        return jnp.dot(jnp.concatenate(left, axis=1), jnp.concatenate(right, axis=0),
                       preferred_element_type=jnp.float32)

    def spread(s, ch):
        for d in range(1, n_row):
            z_copy(s, ch, d).wait_recv()

        def one(d):
            other = lax.rem(chip + d, chips)
            for k in range(2):
                sent[s, ch, d - 1, k] = term(s, ch, other, k).astype(jnp.bfloat16)
            c_copy(s, ch, d).start()

        if chips <= 4:
            for d in range(1, chips):
                one(d)
        else:
            @pl.loop(1, chips)
            def _(d):
                one(d)
        for k in range(2):
            own[ch, k] = term(s, ch, chip, k)

    for s in range(steps):
        if s < 2:
            arrived("rhs", s)
            arrived("diag", s)
        for ch in range(CHUNKS):
            solve(s, ch)
        if s < 2:
            arrived("fac", s)
            if s == 0:
                arrived("cols", 0)
        if s < links:
            for ch in range(CHUNKS):
                spread(s, ch)

    for c in cross.values():
        c.wait_send()
    for s in range(steps):
        for ch in range(CHUNKS):
            keep, give = out_copies(s, ch)
            keep.wait()
            give.wait()
            if s < links:
                for d in range(1, n_row):
                    z_copy(s, ch, d).wait_send()
                for d in range(1, chips):
                    c_copy(s, ch, d).wait_send()


def on_device(n_col, n_row, rhs, diag_inv, factor, columns):
    steps, rows, width = rhs.shape[0], rhs.shape[3], rhs.shape[4]
    targets, slots = factor.shape[3], factor.shape[4]
    chips, half = n_col // 2, width // 2
    wide, links = half // CHUNKS, steps - 1
    bf16 = jnp.bfloat16
    dma = pltpu.SemaphoreType.DMA
    scratch = [
        pltpu.VMEM((steps, 2, rows, half), bf16),
        pltpu.VMEM((steps, 2, rows, rows), bf16),
        pltpu.VMEM((links, 2, targets, slots, rows, rows), bf16),
        pltpu.SMEM(columns.shape, jnp.int32),
        pltpu.VMEM((CHUNKS, 2, rows, wide), jnp.float32),
        pltpu.VMEM((links, CHUNKS, chips - 1, 2, rows, wide), bf16),
        pltpu.VMEM((links, CHUNKS, chips - 1, 2, rows, wide), bf16),
        pltpu.VMEM((CHUNKS, 2, rows, wide), bf16),
        dma((3, 2)), dma((4, 2)), dma((4, 2)),
        dma((links, CHUNKS, n_row - 1)), dma((links, CHUNKS, n_row - 1)),
        dma((links, CHUNKS, chips - 1)), dma((links, CHUNKS, chips - 1)),
        dma((steps, CHUNKS)), dma((steps, CHUNKS)), dma((steps, CHUNKS)),
    ] + [pltpu.VMEM((n_row, 2, rows, wide), bf16) for _ in range(links * CHUNKS)]
    anywhere = pl.BlockSpec(memory_space=pl.ANY)
    return pl.pallas_call(
        functools.partial(kernel, n_col, n_row),
        out_shape=jax.ShapeDtypeStruct(rhs.shape, bf16),
        in_specs=[anywhere, anywhere, anywhere, pl.BlockSpec(memory_space=pltpu.SMEM), anywhere],
        out_specs=anywhere,
        scratch_shapes=scratch,
        compiler_params=pltpu.CompilerParams(
            collective_id=0, has_side_effects=True, vmem_limit_bytes=60 * 1024 * 1024),
        name="levels",
    )(rhs, diag_inv, factor, columns, columns)


def solution(mesh):
    n_col, n_row = mesh.shape["col"], mesh.shape["row"]
    return jax.shard_map(
        functools.partial(on_device, n_col, n_row),
        mesh=mesh,
        in_specs=(
            P(None, "col", "row", None, None),
            P(None, "col", "row", None, None),
            P(None, "col", "row", None, None, None, None),
            P(None, "col", "row", None, None),
        ),
        out_specs=P(None, "col", "row", None, None),
        check_vma=False,
    )
```

time: 324 us -> 85.7 us (0.26)
  waiting for transfers between devices: 184 us -> 0 us
  Pallas kernels: 0 us -> 82 us
  blocking collectives: 78.8 us -> 0 us
  matrix products: 28.3 us -> 0 us
  local copies, waits for them, and re-layouts: 17.3 us -> 3.49 us
  between operations: 13.3 us -> 0.01 us
    reduce_scatter x5 -> x0, waiting for transfers between devices: 184 us -> none  [on_device(): lax.psum_scatter(contrib.astype(jnp.bfloat16), 'col', scatter_dimension=0...]
    pallas_call x0 -> x1, Pallas kernels: none -> 82 us  [on_device(): pl.pallas_call(functools.partial(kernel, n_col, n_row), out_shape=jax.Sha...]
    all_gather x5 -> x0, blocking collectives: 78.8 us -> none  [on_device(): panels = lax.all_gather(current[None], 'row', axis=0, tiled=True)]
    dot_general x11 -> x0, matrix products: 28.3 us -> none  [the longest x5 17.1 us: local_terms(): jnp.einsum('tmab,tmbn->tan', blocks, chosen, preferred_element_type=jnp.f...]
    gather x10 -> x0, local copies, waits for them, and re-layouts: 15.3 us -> none  [local_terms(): chosen = jnp.take(panels, selected, axis=0)]
  transfers between devices with their start and end apart: 5 -> 0, of which waited for: 5 -> 0; matrix products, arithmetic and copies ran while one was open for 1% -> 0% of each run, Pallas kernels for 0% -> 0%
where the time goes in v1:
time: 85.7 us; the launch traced here: 85.5 us
  Pallas kernels  82 us (96%)
  local copies, waits for them, and re-layouts  3.49 us (4%)
    pallas_call x1, Pallas kernels, on_device(): pl.pallas_call(functools.partial(kernel, n_col, n_row), out_shape=jax.Sha...  82 us
    unnamed x2, local copies, waits for them, and re-layouts  3.49 us

profile of v1, /device:TPU:0, one launch (start us, length us, event | category | flops | bytes accessed | tf_op | source)
XLA Modules:
  0.0 85.5 jit_solution(1200323408062400644)
XLA Ops:
  0.0 1.4 %copy.5.cols.cols_hbm = s32[5,1,1,8,2]{4,3,2,1,0:T(8,128)} copy(s32[5,1,1,8,2]{3,4,2,1,0:T(2,128)} %param.7) | data formatting | bytes 640 | tf_op args[3]
  1.4 82.0 %levels.1 = bf16[6,1,1,128,512]{4,3,2,1,0:T(8,128)(2,1)} custom-call(bf16[6,1,1,128,512]{4,3,2,1,0:T(8,128)(2,1)} %rhs.1, bf16[6,1,1,128,128]{4,3,2,1,0:T(8,128)(2,1)} %diag.1, bf16[5,1,1,8,2,128,128]{6,5,4,3,2,1,0:T(8,128)(2,1)} %fac.1, s32[5,1,1,8,2]{4,3,2,1,0:T(8,128)} %copy.5.cols.cols_hbm, s32[5,1,1,8,2]{4,3,2,1,0:T(8,128)} %copy.5.cols.cols_hbm), custom_call_target="tpu_custom_call" | custom-call | tf_op jit(solution)/shard_map/levels/pallas_call | solution.py:215
  83.4 2.1 %copy.8 = bf16[6,1,1,128,512]{4,3,2,1,0:T(8,128)(2,1)} copy(bf16[6,1,1,128,512]{4,3,2,1,0:T(8,128)(2,1)} %levels.1) | data formatting | bytes 1572864

commit v2 on v1

--- a/solution.py
+++ b/solution.py
@@ -9,6 +9,8 @@
 
 MESH = pl.DeviceIdType.MESH
 CHUNKS = 2
+AHEAD = 1
+REACH = (-2, 2, -1, 1)
 
 
 def kernel(n_col, n_row, rhs, diag, fac, cols, cols_hbm, out, *scratch):
@@ -17,9 +19,11 @@
     chips = n_col // 2
     half = width // 2
     wide = half // CHUNKS
+    fold = max(1, 128 // wide)
+    tall = rows // fold
     links = steps - 1
 
-    (rv, dv, fv, cp, own, sent, landed, last,
+    (rv, dv, fv, cp, own, sent, landed, stage,
      in_loc, in_send, in_recv, z_send, z_recv, c_send, c_recv,
      o_loc, o_send, o_recv) = scratch[:18]
     panels = scratch[18:]
@@ -49,12 +53,19 @@
 
     barrier = pltpu.get_barrier_semaphore()
     pl.semaphore_signal(barrier, inc=1, device_id=to(partner, row), device_id_type=MESH)
-    for d in range(1, n_row):
-        pl.semaphore_signal(barrier, inc=1, device_id=to(col, lax.rem(row + d, n_row)), device_id_type=MESH)
+    count = chips
+    for step in REACH:
+        near = (row + step >= 0) & (row + step < n_row)
+        count = count + near.astype(jnp.int32)
+
+        @pl.when(near)
+        def _():
+            pl.semaphore_signal(barrier, inc=1, device_id=to(col, row + step), device_id_type=MESH)
+
     for d in range(1, chips):
         other = lax.rem(chip + d, chips) * 2 + core
         pl.semaphore_signal(barrier, inc=1, device_id=to(other, row), device_id_type=MESH)
-    pl.semaphore_wait(barrier, 1 + n_row - 1 + chips - 1)
+    pl.semaphore_wait(barrier, count)
 
     def remote(src, dst, send, recv, device):
         return pltpu.make_async_remote_copy(
@@ -78,25 +89,66 @@
             local[name, g].wait()
         cross[name, g].wait_recv()
 
+    def pack(x):
+        return x if fold == 1 else jnp.concatenate(
+            [x[i * tall:(i + 1) * tall] for i in range(fold)], axis=1)
+
+    def unpack(x):
+        return x if fold == 1 else jnp.concatenate(
+            [x[:, i * wide:(i + 1) * wide] for i in range(fold)], axis=0)
+
     def part(ch):
         return pl.ds(ch * wide, wide)
 
-    def z_copy(s, ch, d):
+    def z_copy(s, ch, source, step):
         buf = panels[s * CHUNKS + ch]
-        return remote(buf.at[row], buf.at[row], z_send.at[s, ch, d - 1], z_recv.at[s, ch, d - 1],
-                      to(col, lax.rem(row + d, n_row)))
+        way = REACH.index(step)
+        return remote(buf.at[source], buf.at[source], z_send.at[s, ch, way, source],
+                      z_recv.at[s, ch, source], to(col, row + step))
+
+    def reaches(step):
+        return (row + step >= 0) & (row + step < n_row)
+
+    def z_own(s, ch):
+        for step in REACH:
+            @pl.when(reaches(step))
+            def _():
+                z_copy(s, ch, row, step).start()
+
+    def hop(s, ch, h):
+        if h >= n_row:
+            return
+        for _ in (0,):
+            for step in (-1, 1):
+                @pl.when(reaches(-step * h))
+                def _():
+                    z_copy(s, ch, row - step * h, step).wait_recv()
+                    if 2 <= h < n_row - 1:
+                        @pl.when(reaches(step))
+                        def _():
+                            z_copy(s, ch, row - step * h, step).start()
+
+    def z_sent(s, ch):
+        for _ in (0,):
+            for step in REACH:
+                @pl.when(reaches(step))
+                def _():
+                    z_copy(s, ch, row, step).wait_send()
+            for h in range(2, n_row - 1):
+                for step in (-1, 1):
+                    @pl.when(reaches(step) & reaches(-step * h))
+                    def _():
+                        z_copy(s, ch, row - step * h, step).wait_send()
 
     def c_copy(s, ch, d):
         other = lax.rem(chip + d, chips) * 2 + core
         return remote(sent.at[s, ch, d - 1], landed.at[s, ch, d - 1], c_send.at[s, ch, d - 1],
                       c_recv.at[s, ch, d - 1], to(other, row))
 
-    def held(s, ch):
-        return panels[s * CHUNKS + ch].at[row] if s < links else last.at[ch]
-
     def out_copies(s, ch):
-        span = pl.ds(pl.multiple_of(core * half + ch * wide, wide), wide)
-        src = held(s, ch)
+        first, size = (ch + 1 - fold) * wide, fold * wide
+        span = pl.ds(pl.multiple_of(core * half + first, size), size)
+        src = stage.at[s, :, :, pl.ds(first, size)]
         keep = pltpu.make_async_copy(src.at[0], out.at[s, 0, 0, :, span], o_loc.at[s, ch])
         give = remote(src.at[1], out.at[s, 0, 0, :, span], o_send.at[s, ch], o_recv.at[s, ch], pair)
         return keep, give
@@ -113,7 +165,7 @@
             else:
                 total = own[ch, k]
                 for d in range(1, chips):
-                    total = total + landed[s - 1, ch, d - 1, k].astype(jnp.float32)
+                    total = total + unpack(landed[s - 1, ch, d - 1, k]).astype(jnp.float32)
                 rem = right.astype(jnp.float32) - total
                 high = rem.astype(jnp.bfloat16)
                 low = (rem - high.astype(jnp.float32)).astype(jnp.bfloat16)
@@ -122,14 +174,13 @@
                             preferred_element_type=jnp.float32)
             x = x.astype(jnp.bfloat16)
             if s < links:
-                panels[s * CHUNKS + ch][row, k] = x
-            else:
-                last[ch, k] = x
+                panels[s * CHUNKS + ch][row, k] = pack(x)
+            stage[s, k, :, part(ch)] = x
         if s < links:
-            for d in range(1, n_row):
-                z_copy(s, ch, d).start()
-        for c in out_copies(s, ch):
-            c.start()
+            z_own(s, ch)
+        if ch % fold == fold - 1:
+            for c in out_copies(s, ch):
+                c.start()
 
     def term(s, ch, other, k):
         buf = panels[s * CHUNKS + ch]
@@ -138,18 +189,15 @@
         for slot, index in ((0, cols), (1, cp)):
             for m in range(slots):
                 left.append(fv[s, slot, t, m])
-                right.append(buf[index[s, 0, 0, t, m], slot])
+                right.append(unpack(buf[index[s, 0, 0, m, t], slot]))
         return jnp.dot(jnp.concatenate(left, axis=1), jnp.concatenate(right, axis=0),
                        preferred_element_type=jnp.float32)
 
     def spread(s, ch):
-        for d in range(1, n_row):
-            z_copy(s, ch, d).wait_recv()
-
         def one(d):
             other = lax.rem(chip + d, chips)
             for k in range(2):
-                sent[s, ch, d - 1, k] = term(s, ch, other, k).astype(jnp.bfloat16)
+                sent[s, ch, d - 1, k] = pack(term(s, ch, other, k).astype(jnp.bfloat16))
             c_copy(s, ch, d).start()
 
         if chips <= 4:
@@ -162,39 +210,49 @@
         for k in range(2):
             own[ch, k] = term(s, ch, chip, k)
 
+    def ready(s, names):
+        if s < 2:
+            for name in names:
+                arrived(name, s)
+
     for s in range(steps):
-        if s < 2:
-            arrived("rhs", s)
-            arrived("diag", s)
+        ready(s, ("rhs", "diag"))
         for ch in range(CHUNKS):
             solve(s, ch)
-        if s < 2:
-            arrived("fac", s)
-            if s == 0:
-                arrived("cols", 0)
         if s < links:
+            ready(s, ("fac", "cols") if s == 0 else ("fac",))
+            for ch in range(AHEAD):
+                hop(s, ch, 2)
             for ch in range(CHUNKS):
+                if ch + AHEAD < CHUNKS:
+                    hop(s, ch + AHEAD, 2)
+                for h in range(3, n_row):
+                    hop(s, ch, h)
+                hop(s, ch, 1)
                 spread(s, ch)
 
     for c in cross.values():
         c.wait_send()
     for s in range(steps):
         for ch in range(CHUNKS):
-            keep, give = out_copies(s, ch)
-            keep.wait()
-            give.wait()
+            if ch % fold == fold - 1:
+                keep, give = out_copies(s, ch)
+                keep.wait()
+                give.wait()
             if s < links:
-                for d in range(1, n_row):
-                    z_copy(s, ch, d).wait_send()
+                z_sent(s, ch)
                 for d in range(1, chips):
                     c_copy(s, ch, d).wait_send()
 
 
 def on_device(n_col, n_row, rhs, diag_inv, factor, columns):
     steps, rows, width = rhs.shape[0], rhs.shape[3], rhs.shape[4]
+    columns = jnp.swapaxes(columns, 3, 4)
     targets, slots = factor.shape[3], factor.shape[4]
     chips, half = n_col // 2, width // 2
     wide, links = half // CHUNKS, steps - 1
+    fold = max(1, 128 // wide)
+    packed = (rows // fold, wide * fold)
     bf16 = jnp.bfloat16
     dma = pltpu.SemaphoreType.DMA
     scratch = [
@@ -203,14 +261,14 @@
         pltpu.VMEM((links, 2, targets, slots, rows, rows), bf16),
         pltpu.SMEM(columns.shape, jnp.int32),
         pltpu.VMEM((CHUNKS, 2, rows, wide), jnp.float32),
-        pltpu.VMEM((links, CHUNKS, chips - 1, 2, rows, wide), bf16),
-        pltpu.VMEM((links, CHUNKS, chips - 1, 2, rows, wide), bf16),
-        pltpu.VMEM((CHUNKS, 2, rows, wide), bf16),
+        pltpu.VMEM((links, CHUNKS, chips - 1, 2) + packed, bf16),
+        pltpu.VMEM((links, CHUNKS, chips - 1, 2) + packed, bf16),
+        pltpu.VMEM((steps, 2, rows, half), bf16),
         dma((3, 2)), dma((4, 2)), dma((4, 2)),
-        dma((links, CHUNKS, n_row - 1)), dma((links, CHUNKS, n_row - 1)),
+        dma((links, CHUNKS, len(REACH), n_row)), dma((links, CHUNKS, n_row)),
         dma((links, CHUNKS, chips - 1)), dma((links, CHUNKS, chips - 1)),
         dma((steps, CHUNKS)), dma((steps, CHUNKS)), dma((steps, CHUNKS)),
-    ] + [pltpu.VMEM((n_row, 2, rows, wide), bf16) for _ in range(links * CHUNKS)]
+    ] + [pltpu.VMEM((n_row, 2) + packed, bf16) for _ in range(links * CHUNKS)]
     anywhere = pl.BlockSpec(memory_space=pl.ANY)
     return pl.pallas_call(
         functools.partial(kernel, n_col, n_row),

time: 85.7 us -> 81.6 us (0.952)
  Pallas kernels: 82 us -> 79.4 us
  local copies, waits for them, and re-layouts: 3.49 us -> 2.1 us
    pallas_call x1, Pallas kernels: 82 us -> 79.4 us  [on_device(): pl.pallas_call(functools.partial(kernel, n_col, n_row), out_shape=jax.Sha...]
    unnamed x2 -> x1, local copies, waits for them, and re-layouts: 3.49 us -> 2.1 us
where the time goes in v2:
time: 81.6 us; the launch traced here: 81.5 us
  Pallas kernels  79.4 us (97%)
  local copies, waits for them, and re-layouts  2.1 us (3%)
    pallas_call x1, Pallas kernels, on_device(): pl.pallas_call(functools.partial(kernel, n_col, n_row), out_shape=jax.Sha...  79.4 us
    unnamed x1, local copies, waits for them, and re-layouts  2.1 us

profile of v2, /device:TPU:0, one launch (start us, length us, event | category | flops | bytes accessed | tf_op | source)
XLA Modules:
  0.0 81.5 jit_solution(17173323946170289285)
XLA Ops:
  0.0 79.4 %levels.1 = bf16[6,1,1,128,512]{4,3,2,1,0:T(8,128)(2,1)} custom-call(bf16[6,1,1,128,512]{4,3,2,1,0:T(8,128)(2,1)} %rhs.1, bf16[6,1,1,128,128]{4,3,2,1,0:T(8,128)(2,1)} %diag.1, bf16[5,1,1,8,2,128,128]{6,5,4,3,2,1,0:T(8,128)(2,1)} %fac.1, s32[5,1,1,2,8]{4,3,2,1,0:T(2,128)} %bitcast.1, s32[5,1,1,2,8]{4,3,2,1,0:T(2,128)} %bitcast.2), custom_call_target="tpu_custom_call" | custom-call | tf_op jit(solution)/shard_map/levels/pallas_call | solution.py:273
  79.4 2.1 %copy.6 = bf16[6,1,1,128,512]{4,3,2,1,0:T(8,128)(2,1)} copy(bf16[6,1,1,128,512]{4,3,2,1,0:T(8,128)(2,1)} %levels.1) | data formatting | bytes 1572864
